TPU v7x, 32 devices: a whole 2x2x4 slice. The times are simulated.
32 devices in a mesh: wide: 8 (over y, x, core), narrow: 4 (over z).
Axes of the slice: x: 2, y: 2, z: 4, core: 2. Of those that a mesh axis runs over, the one named last changes fastest.
Arguments:
- pooled: bfloat16 [16384, 1024], P(('wide', 'narrow')), may hold values from -6 to 6
- cotangent: bfloat16 [16384, 512], P(('wide', 'narrow')), may hold values from -6 to 6
- w_first: bfloat16 [1024, 1024], P('narrow'), may hold values from -0.1875 to 0.1875
- b_first: float32 [1024], replicated, may hold values from -5 to 5
- w_second: bfloat16 [1024, 512], P('narrow'), may hold values from -0.1875 to 0.1875
- counts: bfloat16 [8, 64, 16384], P(None, 'narrow', 'wide'), may hold values from 0 to 3, as said below
- row_ids: int32 [8, 64], P(None, 'narrow'), may hold values from 0 to 63, as said below
- table: float32 [8, 256, 128], P(None, 'narrow'), may hold values from -6 to 6
- accum: float32 [8, 256, 128], P(None, 'narrow'), may hold values from 0.1 to 10
Outputs:
- new_table: float32 [8, 256, 128], P(None, 'narrow')
- new_accum: float32 [8, 256, 128], P(None, 'narrow')
Inputs may be any that keep to these rules, and one draw needn't show every extreme that they name: `counts`: each entry is zero where the sample does not look up the active row, else a positive lookup weight. `row_ids`: for each table, the 16 ids of one owner (slots j * 16 to (j + 1) * 16 - 1) are distinct.
All inputs are finite; a program needn't handle non-finite values.
Results may differ from a plain program's by a relative error of at most 0.0038.
Values may be sent and summed in bfloat16 or wider, within the bound.
A program may use at most 128 MiB of HBM per device.

v0:
```python
import math
import jax
import jax.numpy as jnp
from jax import lax
from jax.sharding import PartitionSpec as P

clip_factor = 0.5
learn_rate = 0.05
epsilon = 1e-08


def tower_back(inputs, cotangent, w_first, b_first, w_second):
    hidden_in = jnp.dot(inputs, w_first, preferred_element_type=jnp.float32) + b_first
    back_hidden = lax.dot_general(
        cotangent, w_second, (((1,), (1,)), ((), ())), preferred_element_type=jnp.float32
    )
    sigmoid_val = jax.nn.sigmoid(hidden_in)
    slopes = sigmoid_val * (1.0 + hidden_in * (1.0 - sigmoid_val))
    deltas = (back_hidden * slopes).astype(jnp.bfloat16)
    return lax.dot_general(
        deltas, w_first, (((1,), (1,)), ((), ())), preferred_element_type=jnp.float32
    ).astype(jnp.bfloat16)


def clip_rows(grads, limit):
    norms = jnp.sqrt(jnp.sum(grads * grads, axis=-1, keepdims=True))
    return grads * (limit / jnp.maximum(norms, limit))


def adagrad_rows(current, old_acc, summed):
    new_acc = old_acc + summed * summed
    return (current - learn_rate * summed / (jnp.sqrt(new_acc) + epsilon), new_acc)


def shards(pooled, cotangent, w_first, b_first, w_second, counts, row_ids, table, accum):
    full_first, full_second = (
        lax.all_gather(w_first, "narrow", axis=0, tiled=True),
        lax.all_gather(w_second, "narrow", axis=0, tiled=True),
    )
    grad_in = tower_back(pooled, cotangent, full_first, b_first, full_second)
    tables = counts.shape[0]
    slots = counts.shape[1]
    bags = counts.shape[2]
    emb = table.shape[2]
    samples = pooled.shape[0]
    scale = 1.0 / math.sqrt(bags)
    limit = clip_factor * math.sqrt(emb)
    regrouped = lax.all_to_all(counts, "narrow", split_axis=2, concat_axis=1, tiled=True)
    local_grad = grad_in.reshape(samples, tables, emb)
    grads = lax.psum_scatter(
        jnp.einsum(
            "tab,btd->atd", regrouped, local_grad, preferred_element_type=jnp.float32
        ).reshape(slots * lax.axis_size("narrow"), tables * emb),
        "narrow",
        scatter_dimension=0,
        tiled=True,
    ).reshape(slots, tables, emb)
    clipped = clip_rows(grads * scale, limit)
    table_index = jnp.arange(tables, dtype=jnp.int32)[:, None]
    current = jnp.transpose(table[table_index, row_ids], (1, 0, 2))
    old_acc = jnp.transpose(accum[table_index, row_ids], (1, 0, 2))
    summed = lax.psum(clipped, "wide")
    new_rows, new_acc = adagrad_rows(current, old_acc, summed)
    new_table = table.at[table_index, row_ids].set(jnp.transpose(new_rows, (1, 0, 2)))
    new_accum = accum.at[table_index, row_ids].set(jnp.transpose(new_acc, (1, 0, 2)))
    return (new_table, new_accum)


def solution(mesh):
    in_specs = (
        P(("wide", "narrow"), None),
        P(("wide", "narrow"), None),
        P("narrow", None),
        P(),
        P("narrow", None),
        P(None, "narrow", "wide"),
        P(None, "narrow"),
        P(None, "narrow", None),
        P(None, "narrow", None),
    )
    out_specs = (P(None, "narrow", None), P(None, "narrow", None))
    return jax.shard_map(shards, mesh=mesh, in_specs=in_specs, out_specs=out_specs, check_vma=False)
```

profile of v0, /device:TPU:0, one launch (start us, length us, event | category | flops | bytes accessed | tf_op | source)
XLA Modules:
  0.0 199.6 jit_solution(9209073839710677612)
XLA Ops:
  7.2 0.0 copy-start
  7.2 0.0 copy-start.3
  7.2 0.0 all-gather.5.cloned.1.call-start
  7.2 1.1 copy.53
  8.3 0.9 copy.54
  9.3 0.0 all-gather.5.cloned.1.call-update
  9.3 0.0 all-gather.3.cloned.1.call-start
  9.3 0.7 all-gather.3.cloned.1.call-update
  10.0 0.0 reduce-scatter.2.cloned.1.call-start
  10.1 0.0 copy-done.3
  10.1 4.2 %copy.26 = bf16[8,16,2048]{1,0,2:T(8,128)(2,1)} copy(bf16[8,16,2048]{2,1,0:T(8,128)(2,1)S(1)} %copy-done.3) | data formatting | bytes 1048576 | tf_op args[5]
  14.3 5.8 %reshape.51 = bf16[4,2,32768]{2,1,0:T(2,128)(2,1)S(1)} reshape(bf16[2048,8,16]{2,1,0:T(8,128)(2,1)} %bitcast.58) | data formatting | bytes 1048576
  20.1 35.4 %all_to_all.18 = bf16[4,2,32768]{2,1,0:T(2,128)(2,1)S(1)} all-to-all(bf16[4,2,32768]{2,1,0:T(2,128)(2,1)S(1)} %reshape.51), channel_id=1, replica_groups=mesh['wide'=8,'narrow'=4] {'narrow'}, dimensions={0} | all-to-all | bytes 1048576 | tf_op jit(solution)/shard_map/all_to_all | solution.py:48
  55.5 4.1 %reshape.52 = bf16[2048,8,16]{2,1,0:T(8,128)(2,1)} reshape(bf16[4,2,32768]{2,1,0:T(2,128)(2,1)S(1)} %all_to_all.18) | data formatting | bytes 1048576
  59.7 4.4 %copy.27 = bf16[8,16,4,512]{3,1,2,0:T(8,128)(2,1)S(1)} copy(bf16[8,16,4,512]{1,0,3,2:T(8,128)(2,1)} %bitcast.57) | data formatting | bytes 1048576 | tf_op jit(solution)/shard_map/all_to_all | solution.py:48
  64.1 0.0 copy-start.5
  64.1 5.2 %all-gather.5.cloned.1.call-done = bf16[1024,1024]{1,0:T(8,128)(2,1)} async-done(((bf16[256,1024]{1,0:T(8,128)(2,1)}), bf16[1024,1024]{1,0:T(8,128)(2,1)}) %all-gather.5.cloned.1.call-update) | async-done | bytes 2097168 | tf_op jit(solution)/shard_map/all_gather | solution.py:37
  69.2 0.0 copy-done
  69.2 4.2 %fusion.13 = f32[512,1024]{1,0:T(8,128)} fusion(bf16[512,1024]{1,0:T(8,128)(2,1)S(1)} %copy-done, bf16[1024,1024]{1,0:T(8,128)(2,1)} %all-gather.5.cloned.1.call-done), kind=kOutput, calls=%fused_computation.32 | convolution fusion | flops 1073741824 | bytes 5242880 | tf_op jit(solution)/shard_map/dot_general | solution.py:13
  73.4 24.1 %all-gather.3.cloned.1.call-done = bf16[1024,512]{1,0:T(8,128)(2,1)} async-done(((bf16[256,512]{1,0:T(8,128)(2,1)}), bf16[1024,512]{1,0:T(8,128)(2,1)}) %all-gather.3.cloned.1.call-update) | async-done | bytes 1048592 | tf_op jit(solution)/shard_map/all_gather | solution.py:38
  97.5 0.0 copy-done.5
  97.5 4.6 %fusion = bf16[64,8,8,128]{3,2,1,0:T(8,128)(2,1)S(1)} fusion(bf16[1024,1024]{1,0:T(8,128)(2,1)} %all-gather.5.cloned.1.call-done, f32[512,1024]{1,0:T(8,128)} %fusion.13, bf16[512,512]{1,0:T(8,128)(2,1)} %param.10, bf16[1024,512]{1,0:T(8,128)(2,1)} %all-gather.3.cloned.1.call-done, f32[1024]{0:T(1024)S(1)} %copy-done.5), kind=kOutput, calls=%fused_computation.6 | convolution fusion | flops 1616379904 | bytes 6819840 | tf_op jit(solution)/shard_map/dot_general | solution.py:20
  102.0 0.0 copy-start.4
  102.1 0.3 convolution_bitcast_fusion
  102.4 0.7 copy.47
  103.1 0.0 reduce-scatter.2.cloned.1.call-update
  103.1 0.0 all-reduce.2.cloned.1.call-start
  103.2 19.5 %reduce-scatter.2.cloned.1.call-done = f32[16,1024]{1,0:T(8,128)} async-done(((f32[64,1024]{1,0:T(8,128)}), f32[16,1024]{1,0:T(8,128)}) %reduce-scatter.2.cloned.1.call-update) | async-done | bytes 65552 | tf_op jit(solution)/shard_map/reduce_scatter | solution.py:50
  122.7 0.9 copy.35
  123.6 0.1 multiply_reduce_fusion
  123.7 0.7 bitcast_multiply_fusion
  124.4 0.0 all-reduce.2.cloned.1.call-update
  124.4 0.0 copy-done.4
  124.4 0.1 reshape.27
  124.5 1.2 gather_fusion
  125.7 1.2 gather_fusion.1
  127.0 0.1 reshape.39
  127.1 50.5 %all-reduce.2.cloned.1.call-done = f32[16,8,128]{2,1,0:T(8,128)} async-done(((f32[16,8,128]{2,1,0:T(8,128)}), f32[16,8,128]{2,1,0:T(8,128)}) %all-reduce.2.cloned.1.call-update) | async-done | bytes 65552 | tf_op jit(solution)/shard_map/psum | solution.py:62
  177.6 0.9 fusion.6
  178.6 6.9 %scatter_fusion.1 = f32[8,64,128]{2,1,0:T(8,128)S(1)} fusion(f32[8,64,128]{2,1,0:T(8,128)S(1)} %copy.54, s32[128]{0:T(128)S(1)} %reshape.39, f32[128,128]{1,0:T(8,128)S(1)} %bitcast.64), kind=kCustom, calls=%fused_computation.3 | custom fusion | bytes 197632 | tf_op jit(solution)/shard_map/scatter | solution.py:65
  185.5 0.0 copy-start.2
  185.5 6.9 %scatter_fusion = f32[8,64,128]{2,1,0:T(8,128)S(1)} fusion(f32[8,64,128]{2,1,0:T(8,128)S(1)} %copy.53, s32[128]{0:T(128)S(1)} %reshape.39, f32[128,128]{1,0:T(8,128)S(1)} %bitcast.63), kind=kCustom, calls=%fused_computation.2 | custom fusion | bytes 197632 | tf_op jit(solution)/shard_map/scatter | solution.py:64
  192.4 0.0 copy-done.2
  192.4 0.0 copy-start.1
  192.4 0.7 copy-done.1
  (5 shorter events, 0.1 us)
Async XLA Ops:
  7.2 62.1 %copy-start = (bf16[512,1024]{1,0:T(8,128)(2,1)S(1)}, bf16[512,1024]{1,0:T(8,128)(2,1)}, u32[]{:S(2)}) copy-start(bf16[512,1024]{1,0:T(8,128)(2,1)} %param.9) | copy-start | bytes 3145732
  7.2 2.9 %copy-start.3 = (bf16[8,16,2048]{2,1,0:T(8,128)(2,1)S(1)}, bf16[8,16,2048]{2,1,0:T(8,128)(2,1)}, u32[]{:S(2)}) copy-start(bf16[8,16,2048]{2,1,0:T(8,128)(2,1)} %param.14) | copy-start | bytes 1572868
  7.2 62.0 %all-gather.5.cloned.1.call-start = ((), (), s32[]{:S(2)}) async-start(), calls=%async_computation.3 | async-start | bytes 2621440 | tf_op jit(solution)/shard_map/all_gather | solution.py:37
  9.3 88.2 %all-gather.3.cloned.1.call-start = ((), (), s32[]{:S(2)}) async-start(), calls=%async_computation.2 | async-start | bytes 1310720 | tf_op jit(solution)/shard_map/all_gather | solution.py:38
  10.0 112.6 %reduce-scatter.2.cloned.1.call-start = ((), (), s32[]{:S(2)}) async-start(), calls=%async_computation.4 | async-start | bytes 327680 | tf_op jit(solution)/shard_map/reduce_scatter | solution.py:50
  64.1 33.4 %copy-start.5 = (f32[1024]{0:T(1024)S(1)}, f32[1024]{0:T(1024)}, u32[]{:S(2)}) copy-start(f32[1024]{0:T(1024)} %param.12) | copy-start | bytes 12292
  102.0 22.4 %copy-start.4 = (s32[8,16]{1,0:T(8,128)S(1)}, s32[8,16]{1,0:T(8,128)}, u32[]{:S(2)}) copy-start(s32[8,16]{1,0:T(8,128)} %param.15) | copy-start | bytes 1540
  103.1 74.5 %all-reduce.2.cloned.1.call-start = ((), (), s32[]{:S(2)}) async-start(), calls=%async_computation.5 | async-start | bytes 131072 | tf_op jit(solution)/shard_map/psum | solution.py:62
  185.5 6.9 %copy-start.2 = (f32[8,64,128]{2,1,0:T(8,128)}, f32[8,64,128]{2,1,0:T(8,128)S(1)}, u32[]{:S(2)}) copy-start(f32[8,64,128]{2,1,0:T(8,128)S(1)} %scatter_fusion.1) | copy-start | bytes 786436
  192.4 0.7 copy-start.1
Sparse Core Ops, SparseCore 0:
  9.6 59.6 all-gather.4
  70.8 26.6 all-gather.2
  103.3 19.3 reduce-scatter.1
  126.2 51.3 all-reduce.1
where the time goes:
time: 200 us
  waiting for transfers between devices  100 us (50%)
  local copies, waits for them, and re-layouts  39.3 us (20%)
  blocking collectives  35.4 us (18%)
  between operations  13.9 us (7%)
  matrix products  9.06 us (5%)
    psum x1, waiting for transfers between devices, shards(): summed = lax.psum(clipped, 'wide')  50.5 us
    all_to_all x1, blocking collectives, shards(): lax.all_to_all(counts, 'narrow', split_axis=2, concat_axis=1, tiled=True)  35.4 us
    all_gather x1, waiting for transfers between devices, shards(): lax.all_gather(w_second, 'narrow', axis=0, tiled=True)  24.1 us
    reduce_scatter x1, waiting for transfers between devices, shards(): lax.psum_scatter(jnp.einsum('tab,btd->atd', regrouped, local_grad, prefer...  19.5 us
    unnamed x18, local copies, waits for them, and re-layouts  17.7 us
    scatter x1, local copies, waits for them, and re-layouts, shards(): accum.at[table_index, row_ids].set(jnp.transpose(new_acc, (1, 0, 2)))  6.9 us
    scatter x1, local copies, waits for them, and re-layouts, shards(): table.at[table_index, row_ids].set(jnp.transpose(new_rows, (1, 0, 2)))  6.9 us
    all_gather x1, waiting for transfers between devices, shards(): lax.all_gather(w_first, 'narrow', axis=0, tiled=True)  5.15 us
  transfers between devices with their start and end apart: 4, of which 4 were waited for; matrix products, arithmetic and copies ran while one was open for 13% of the time, Pallas kernels for 0%

commit v1 on v0

--- a/solution.py
+++ b/solution.py
@@ -45,7 +45,12 @@
     samples = pooled.shape[0]
     scale = 1.0 / math.sqrt(bags)
     limit = clip_factor * math.sqrt(emb)
-    regrouped = lax.all_to_all(counts, "narrow", split_axis=2, concat_axis=1, tiled=True)
+    regrouped = jnp.concatenate(
+        lax.all_to_all(
+            jnp.stack(jnp.split(counts, lax.axis_size("narrow"), axis=2)), "narrow", 0, 0
+        ),
+        axis=1,
+    )
     local_grad = grad_in.reshape(samples, tables, emb)
     grads = lax.psum_scatter(
         jnp.einsum(

time: 200 us -> 196 us (0.980)
  local copies, waits for them, and re-layouts: 39.3 us -> 20.9 us
  waiting for transfers between devices: 100 us -> 118 us
  blocking collectives: 35.4 us -> 32.5 us
    all_gather x1, waiting for transfers between devices: 5.15 us -> 22.4 us  [shards(): lax.all_gather(w_first, 'narrow', axis=0, tiled=True)]
    unnamed x18 -> x15, local copies, waits for them, and re-layouts: 17.7 us -> 3.61 us
    all_to_all x1 -> x0, local copies, waits for them, and re-layouts: 4.4 us -> none  [shards(): lax.all_to_all(counts, 'narrow', split_axis=2, concat_axis=1, tiled=True)]
    all_to_all x1, blocking collectives: 35.4 us -> 32.5 us  [shards(): lax.all_to_all(jnp.stack(jnp.split(counts, lax.axis_size('narrow'), axis=...]
  transfers between devices with their start and end apart: 4 -> 4, of which waited for: 4 -> 4; matrix products, arithmetic and copies ran while one was open for 13% -> 4% of each run, Pallas kernels for 0% -> 0%
where the time goes in v1:
time: 196 us
  waiting for transfers between devices  118 us (60%)
  blocking collectives  32.5 us (17%)
  local copies, waits for them, and re-layouts  20.9 us (11%)
  between operations  13.9 us (7%)
  matrix products  9.02 us (5%)
    psum x1, waiting for transfers between devices, shards(): summed = lax.psum(clipped, 'wide')  50.6 us
    all_to_all x1, blocking collectives, shards(): lax.all_to_all(jnp.stack(jnp.split(counts, lax.axis_size('narrow'), axis=...  32.5 us
    all_gather x1, waiting for transfers between devices, shards(): lax.all_gather(w_second, 'narrow', axis=0, tiled=True)  24.5 us
    all_gather x1, waiting for transfers between devices, shards(): lax.all_gather(w_first, 'narrow', axis=0, tiled=True)  22.4 us
    reduce_scatter x1, waiting for transfers between devices, shards(): lax.psum_scatter(jnp.einsum('tab,btd->atd', regrouped, local_grad, prefer...  19.5 us
    scatter x1, local copies, waits for them, and re-layouts, shards(): table.at[table_index, row_ids].set(jnp.transpose(new_rows, (1, 0, 2)))  6.9 us
    scatter x1, local copies, waits for them, and re-layouts, shards(): accum.at[table_index, row_ids].set(jnp.transpose(new_acc, (1, 0, 2)))  6.9 us
    dot_general x1, matrix products, tower_back(): lax.dot_general(deltas, w_first, (((1,), (1,)), ((), ())), preferred_elem...  4.55 us
  transfers between devices with their start and end apart: 4, of which 4 were waited for; matrix products, arithmetic and copies ran while one was open for 4% of the time, Pallas kernels for 0%

profile of v1, /device:TPU:0, one launch (start us, length us, event | category | flops | bytes accessed | tf_op | source)
XLA Modules:
  0.0 196.0 jit_solution(15080549410355503688)
XLA Ops:
  7.2 0.0 copy-start
  7.2 0.0 copy-start.3
  7.2 0.0 all-gather.5.cloned.1.call-start
  7.2 1.1 copy.45
  8.3 0.9 copy.46
  9.3 0.0 all-gather.5.cloned.1.call-update
  9.3 0.0 all-gather.3.cloned.1.call-start
  9.3 0.7 all-gather.3.cloned.1.call-update
  10.0 0.0 reduce-scatter.2.cloned.1.call-start
  10.1 0.0 copy-done.3
  10.1 0.1 slice_bitcast_fusion.3
  10.2 0.1 pad_maximum_fusion
  10.2 32.5 %all_to_all.5 = bf16[4,8,16,512]{3,2,1,0:T(8,128)(2,1)S(1)} all-to-all(bf16[4,8,16,512]{3,2,1,0:T(8,128)(2,1)S(1)} %pad_maximum_fusion), channel_id=1, replica_groups=mesh['wide'=8,'narrow'=4] {'narrow'}, dimensions={0} | all-to-all | bytes 1048576 | tf_op jit(solution)/shard_map/all_to_all | solution.py:49
  42.8 0.0 copy-start.5
  42.8 22.4 %all-gather.5.cloned.1.call-done = bf16[1024,1024]{1,0:T(8,128)(2,1)} async-done(((bf16[256,1024]{1,0:T(8,128)(2,1)}), bf16[1024,1024]{1,0:T(8,128)(2,1)}) %all-gather.5.cloned.1.call-update) | async-done | bytes 2097168 | tf_op jit(solution)/shard_map/all_gather | solution.py:37
  65.1 0.0 copy-done
  65.1 4.1 %fusion.13 = f32[512,1024]{1,0:T(8,128)} fusion(bf16[512,1024]{1,0:T(8,128)(2,1)S(1)} %copy-done, bf16[1024,1024]{1,0:T(8,128)(2,1)} %all-gather.5.cloned.1.call-done), kind=kOutput, calls=%fused_computation.37 | convolution fusion | flops 1073741824 | bytes 5242880 | tf_op jit(solution)/shard_map/dot_general | solution.py:13
  69.3 24.5 %all-gather.3.cloned.1.call-done = bf16[1024,512]{1,0:T(8,128)(2,1)} async-done(((bf16[256,512]{1,0:T(8,128)(2,1)}), bf16[1024,512]{1,0:T(8,128)(2,1)}) %all-gather.3.cloned.1.call-update) | async-done | bytes 1048592 | tf_op jit(solution)/shard_map/all_gather | solution.py:38
  93.8 0.0 copy-done.5
  93.8 4.6 %fusion = bf16[64,8,8,128]{3,2,1,0:T(8,128)(2,1)S(1)} fusion(bf16[1024,1024]{1,0:T(8,128)(2,1)} %all-gather.5.cloned.1.call-done, f32[512,1024]{1,0:T(8,128)} %fusion.13, bf16[512,512]{1,0:T(8,128)(2,1)} %param.10, bf16[1024,512]{1,0:T(8,128)(2,1)} %all-gather.3.cloned.1.call-done, f32[1024]{0:T(1024)S(1)} %copy-done.5), kind=kOutput, calls=%fused_computation.6 | convolution fusion | flops 1616379904 | bytes 6819840 | tf_op jit(solution)/shard_map/dot_general | solution.py:20
  98.4 0.0 copy-start.4
  98.4 0.3 convolution_bitcast_fusion
  98.7 0.7 copy.39
  99.4 0.0 reduce-scatter.2.cloned.1.call-update
  99.5 0.0 all-reduce.2.cloned.1.call-start
  99.5 19.5 %reduce-scatter.2.cloned.1.call-done = f32[16,1024]{1,0:T(8,128)} async-done(((f32[64,1024]{1,0:T(8,128)}), f32[16,1024]{1,0:T(8,128)}) %reduce-scatter.2.cloned.1.call-update) | async-done | bytes 65552 | tf_op jit(solution)/shard_map/reduce_scatter | solution.py:55
  119.0 0.9 copy.27
  119.9 0.1 multiply_reduce_fusion
  120.0 0.7 bitcast_multiply_fusion
  120.7 0.0 all-reduce.2.cloned.1.call-update
  120.7 0.0 copy-done.4
  120.7 0.1 reshape.35
  120.8 1.2 gather_fusion
  122.1 1.2 gather_fusion.1
  123.3 0.1 reshape.47
  123.4 50.6 %all-reduce.2.cloned.1.call-done = f32[16,8,128]{2,1,0:T(8,128)} async-done(((f32[16,8,128]{2,1,0:T(8,128)}), f32[16,8,128]{2,1,0:T(8,128)}) %all-reduce.2.cloned.1.call-update) | async-done | bytes 65552 | tf_op jit(solution)/shard_map/psum | solution.py:67
  173.9 0.9 fusion.6
  174.9 6.9 %scatter_fusion.1 = f32[8,64,128]{2,1,0:T(8,128)S(1)} fusion(f32[8,64,128]{2,1,0:T(8,128)S(1)} %copy.46, s32[128]{0:T(128)S(1)} %reshape.47, f32[128,128]{1,0:T(8,128)S(1)} %bitcast.67), kind=kCustom, calls=%fused_computation.3 | custom fusion | bytes 197632 | tf_op jit(solution)/shard_map/scatter | solution.py:70
  181.8 0.0 copy-start.2
  181.8 6.9 %scatter_fusion = f32[8,64,128]{2,1,0:T(8,128)S(1)} fusion(f32[8,64,128]{2,1,0:T(8,128)S(1)} %copy.45, s32[128]{0:T(128)S(1)} %reshape.47, f32[128,128]{1,0:T(8,128)S(1)} %bitcast.66), kind=kCustom, calls=%fused_computation.2 | custom fusion | bytes 197632 | tf_op jit(solution)/shard_map/scatter | solution.py:69
  188.7 0.0 copy-done.2
  188.7 0.0 copy-start.1
  188.7 0.7 copy-done.1
  (6 shorter events, 0.1 us)
Async XLA Ops:
  7.2 58.0 %copy-start = (bf16[512,1024]{1,0:T(8,128)(2,1)S(1)}, bf16[512,1024]{1,0:T(8,128)(2,1)}, u32[]{:S(2)}) copy-start(bf16[512,1024]{1,0:T(8,128)(2,1)} %param.9) | copy-start | bytes 3145732
  7.2 2.9 %copy-start.3 = (bf16[8,16,2048]{2,1,0:T(8,128)(2,1)S(1)}, bf16[8,16,2048]{2,1,0:T(8,128)(2,1)}, u32[]{:S(2)}) copy-start(bf16[8,16,2048]{2,1,0:T(8,128)(2,1)} %param.14) | copy-start | bytes 1572868
  7.2 57.9 %all-gather.5.cloned.1.call-start = ((), (), s32[]{:S(2)}) async-start(), calls=%async_computation.3 | async-start | bytes 2621440 | tf_op jit(solution)/shard_map/all_gather | solution.py:37
  9.3 84.5 %all-gather.3.cloned.1.call-start = ((), (), s32[]{:S(2)}) async-start(), calls=%async_computation.2 | async-start | bytes 1310720 | tf_op jit(solution)/shard_map/all_gather | solution.py:38
  10.0 109.0 %reduce-scatter.2.cloned.1.call-start = ((), (), s32[]{:S(2)}) async-start(), calls=%async_computation.4 | async-start | bytes 327680 | tf_op jit(solution)/shard_map/reduce_scatter | solution.py:55
  42.8 51.1 %copy-start.5 = (f32[1024]{0:T(1024)S(1)}, f32[1024]{0:T(1024)}, u32[]{:S(2)}) copy-start(f32[1024]{0:T(1024)} %param.12) | copy-start | bytes 12292
  98.4 22.3 %copy-start.4 = (s32[8,16]{1,0:T(8,128)S(1)}, s32[8,16]{1,0:T(8,128)}, u32[]{:S(2)}) copy-start(s32[8,16]{1,0:T(8,128)} %param.15) | copy-start | bytes 1540
  99.5 74.5 %all-reduce.2.cloned.1.call-start = ((), (), s32[]{:S(2)}) async-start(), calls=%async_computation.5 | async-start | bytes 131072 | tf_op jit(solution)/shard_map/psum | solution.py:67
  181.8 6.9 %copy-start.2 = (f32[8,64,128]{2,1,0:T(8,128)}, f32[8,64,128]{2,1,0:T(8,128)S(1)}, u32[]{:S(2)}) copy-start(f32[8,64,128]{2,1,0:T(8,128)S(1)} %scatter_fusion.1) | copy-start | bytes 786436
  188.7 0.7 copy-start.1
Sparse Core Ops, SparseCore 0:
  9.6 55.5 all-gather.4
  66.7 27.0 all-gather.2
  99.6 19.3 reduce-scatter.1
  122.5 51.4 all-reduce.1
